TPU v7x, 128 devices: a whole 4x4x4 slice. The times are simulated.
128 devices in a mesh: leaf: 64 (over z, x, y), sub: 2 (over core).
Axes of the slice: x: 4, y: 4, z: 4, core: 2. Of those that a mesh axis runs over, the one named last changes fastest.
Arguments:
- right_sides: float32 [2, 4, 16, 6144], P(None, None, None, ('leaf', 'sub')), may hold values from -6 to 6
- diag_inverse: float32 [2, 6144, 11520], P(None, ('leaf', 'sub'))
- coupling: float32 [2, 6144, 5376], P(None, ('leaf', 'sub'))
- boundary: int32 [128, 5376], P(('leaf', 'sub')), may hold values from 0 to 10751, as said below
- plane_map: int32 [128, 192], P(('leaf', 'sub')), may hold values from 0 to 191, each once within a row
Outputs:
- plane_field: float32 [2, 16, 24576], P(None, None, ('leaf', 'sub'))
Inputs may be any that keep to these rules, and one draw needn't show every extreme that they name: `boundary`: for level l >= 1 (columns e_l .. e_l + n_l - 1 of a row), entries lie in 0 .. (sum of n_a over a < l) - 1 and are equal on all devices d with the same d div (128 / 2^l); the first entry of each such segment is its largest allowed value and the second is 0.
All inputs are finite; a program needn't handle non-finite values.
Results may differ from a plain program's by a relative error of at most 0.0001.
Values sent between devices are 32-bit elements; how exact they have to be, the bound alone decides.
A program may use at most 64 MiB of HBM per device.

v0:
```python
import functools

import jax
import jax.numpy as jnp
from jax import lax
from jax.experimental import pallas as pl
from jax.experimental.pallas import tpu as pltpu
from jax.sharding import PartitionSpec as P

LEVELS = 4
GROUPS = 3
LANES = 128
MESH = pl.DeviceIdType.MESH
F32, BF16 = jnp.float32, jnp.bfloat16


def lane(rows):
    return lax.broadcasted_iota(jnp.int32, (rows, LANES), 1)


def roll(x, by):
    return pltpu.roll(x, by % LANES, 1)


def split(x):
    hi = x.astype(BF16)
    return hi, (x - hi.astype(F32)).astype(BF16)


def product(hi, lo, values):
    vhi, vlo = split(values)
    both = jnp.dot(hi, jnp.concatenate([vhi, vlo], axis=1), preferred_element_type=F32)
    rest = jnp.dot(lo, vhi, preferred_element_type=F32)
    return both[:, :LANES] + both[:, LANES:] + rest


def fold(t, rows, width):
    half = width // 2
    m = 2 * rows
    y = t[:m] + roll(t[m : 2 * m], -width) + roll(t[2 * m :], -2 * width)
    a, b = y[:rows], y[rows:]
    at = lane(rows)
    swapped = jnp.where(at < half, -roll(b, -half), roll(b, half))
    return a + swapped


def pack(x, part, width):
    at = lane(part)
    return jnp.where(
        at < width,
        x[:part],
        jnp.where(
            at < 2 * width, roll(x[part : 2 * part], width), roll(x[2 * part :], 2 * width)
        ),
    )


def repeat(x, at, group, width):
    v = jnp.where((at >= group * width) & (at < (group + 1) * width), x, 0.0)
    v = v + roll(v, width)
    return v + roll(v, 2 * width)


def body(
    chips, rows, orders, rs, d_hbm, u_hbm, bnd, pm, out, dv, uv, dp, up, perm, *rest
):
    bufs, (xu, bg, rt, sol, snd, rcv, load_sem, send_sem, recv_sem) = rest[:7], rest[7:]
    leaf, sub = lax.axis_index("leaf"), lax.axis_index("sub")
    part = rows // GROUPS
    width = rs.shape[0] * rs.shape[2]
    d_at = [sum(orders[:a]) for a in range(LEVELS + 1)]
    u_at = [0] + [sum(orders[1:a]) for a in range(1, LEVELS + 1)]

    loads = []
    for level in range(LEVELS):
        span = pl.ds(d_at[level], orders[level])
        loads.append(
            pltpu.make_async_copy(d_hbm.at[:, :, span], dv.at[:, :, span], load_sem.at[level])
        )
    loads.append(pltpu.make_async_copy(u_hbm, uv, load_sem.at[LEVELS]))
    for load in loads:
        load.start()

    def block(level):
        count = chips >> level
        return count, lax.rem(leaf, count), leaf - lax.rem(leaf, count)

    def send(stage, level, packed):
        buf = bufs[stage]
        count, mine, base = block(level)
        buf[sub, mine] = packed

        def one(k, carry):
            pltpu.make_async_remote_copy(
                src_ref=buf.at[sub, mine],
                dst_ref=buf.at[sub, mine],
                send_sem=send_sem.at[stage],
                recv_sem=recv_sem.at[stage],
                device_id=(base + lax.rem(mine + k, count), sub),
                device_id_type=MESH,
            ).start()
            return carry

        lax.fori_loop(1, count, one, 0)

    def forward(stage, level):
        buf = bufs[stage]
        count, _, _ = block(level)
        some = buf.at[sub, pl.ds(0, count - 1)]
        pltpu.make_async_copy(some, some, recv_sem.at[stage]).wait()
        copy = pltpu.make_async_remote_copy(
            src_ref=buf.at[sub],
            dst_ref=buf.at[sub],
            send_sem=send_sem.at[8 + stage],
            recv_sem=recv_sem.at[8 + stage],
            device_id=(leaf, 1 - sub),
            device_id_type=MESH,
        )
        copy.start()
        return copy

    def arrived(stage):
        other = bufs[stage].at[1 - sub]
        pltpu.make_async_copy(other, other, recv_sem.at[8 + stage]).wait()

    def prepare_diag(level):
        loads[level].wait()
        chunk = perm.shape[0]
        half = orders[level] // (2 * GROUPS)
        base = d_at[level] // GROUPS
        for t in range(orders[level] // chunk):
            at = d_at[level] + t * chunk
            hi, lo = split(dv[:, :, at : at + chunk].reshape(2 * rows, chunk))
            both = jnp.concatenate([hi, lo], axis=0)
            moved = jnp.dot(both, perm[...], preferred_element_type=F32).astype(BF16)
            for p in range(2):
                for g in range(GROUPS):
                    to = base + p * half + t * LANES
                    frm = (p * GROUPS + g) * LANES
                    for h in range(2):
                        dp[h, g, :, to : to + LANES] = moved[
                            h * 2 * rows : (h + 1) * 2 * rows, frm : frm + LANES
                        ]

    def prepare_coupling(level):
        k = orders[level] // GROUPS
        base = u_at[level] // GROUPS
        for g in range(GROUPS):
            at = u_at[level] + g * k
            hi, lo = split(uv[:, :, at : at + k].reshape(2 * rows, k))
            up[0, g, :, base : base + k] = hi
            up[1, g, :, base : base + k] = lo

    def diag_product(stage, level):
        buf = bufs[stage]
        half = orders[level] // (2 * GROUPS)
        base = d_at[level] // GROUPS
        copy = forward(stage, level)

        def part_of(p):
            at = pl.ds(pl.multiple_of(base + p * half, LANES), half)
            return product(
                dp[0, :, :, at].reshape(GROUPS * 2 * rows, half),
                dp[1, :, :, at].reshape(GROUPS * 2 * rows, half),
                buf[p].reshape(half, LANES),
            )

        total = part_of(sub)
        arrived(stage)
        total = total + part_of(1 - sub)
        copy.wait_send()
        return fold(total, rows, width)

    def collect(stage, level):
        buf = bufs[stage]
        count, _, _ = block(level)
        copy = forward(stage, level)
        at = lane(part)

        def spread(p):
            def one(c, carry):
                v = buf[p, c]
                for g in range(GROUPS):
                    to = d_at[level] + c * 2 * rows + p * rows + g * part
                    xu[pl.ds(pl.multiple_of(to, 16), part), :] = repeat(v, at, g, width)
                return carry

            lax.fori_loop(0, count, one, 0, unroll=4)

        spread(sub)
        arrived(stage)
        spread(1 - sub)
        copy.wait_send()

    def coupling_product(level):
        k = orders[level] // GROUPS
        at = lane(1)

        def one(i, carry):
            for u in range(8):
                j = i * 8 + u
                r = [
                    xu[pl.ds(bnd[0, u_at[level] + g * k + j], 1), :] for g in range(GROUPS)
                ]
                bg[pl.ds(j, 1), :] = jnp.where(
                    at < width, r[0], jnp.where(at < 2 * width, r[1], r[2])
                )
            return carry

        lax.fori_loop(0, k // 8, one, 0)
        base = u_at[level] // GROUPS
        return fold(
            product(
                up[0, :, :, base : base + k].reshape(GROUPS * 2 * rows, k),
                up[1, :, :, base : base + k].reshape(GROUPS * 2 * rows, k),
                bg[:k],
            ),
            rows,
            width,
        )

    def keep(level, x):
        sol[level * rows : (level + 1) * rows, :] = repeat(x, lane(rows), 0, width)

    for level in range(LEVELS):
        rt[level, :, :width] = jnp.transpose(rs[:, level].reshape(width, rows))
    send(0, 0, pack(rt[0], part, width))

    chunk = perm.shape[0]
    col = lax.broadcasted_iota(jnp.int32, (1, chunk), 1)
    block_at = jnp.right_shift(col, 7)
    second = (block_at >= GROUPS).astype(jnp.int32)
    source = (
        jnp.right_shift(col & 127, 4) * (2 * rows)
        + second * rows
        + (block_at - GROUPS * second) * part
        + (col & 15)
    )
    row = lax.broadcasted_iota(jnp.int32, (chunk, chunk), 0)
    perm[...] = jnp.where(row == source, 1.0, 0.0).astype(BF16)

    prepare_diag(0)
    x = diag_product(0, 0)
    keep(0, x)
    send(1, 0, pack(x, part, width))
    loads[LEVELS].wait()
    for level in range(1, LEVELS):
        prepare_coupling(level)
        prepare_diag(level)
    for level in range(1, LEVELS):
        collect(2 * level - 1, level - 1)
        z = rt[level] - coupling_product(level)
        send(2 * level, level, pack(z, part, width))
        x = diag_product(2 * level, level)
        keep(level, x)
        if level + 1 < LEVELS:
            send(2 * level + 1, level, pack(x, part, width))

    at = lane(1)

    def pick(j, carry):
        r = [sol[pl.ds(pm[0, GROUPS * j + p], 1), :] for p in range(GROUPS)]
        snd[j] = jnp.where(at < width, r[0], jnp.where(at < 2 * width, r[1], r[2]))
        return carry

    lax.fori_loop(0, chips, pick, 0, unroll=8)
    rcv[leaf] = snd[leaf]

    def one(k, carry):
        to = lax.rem(leaf + k, chips)
        pltpu.make_async_remote_copy(
            src_ref=snd.at[to],
            dst_ref=rcv.at[leaf],
            send_sem=send_sem.at[7],
            recv_sem=recv_sem.at[7],
            device_id=(to, sub),
            device_id_type=MESH,
        ).start()
        return carry

    lax.fori_loop(1, chips, one, 0)
    some = rcv.at[pl.ds(0, chips - 1)]
    pltpu.make_async_copy(some, some, recv_sem.at[7]).wait()
    got = rcv[...].reshape(chips, LANES)
    frm = lax.broadcasted_iota(jnp.int32, (chips, GROUPS * chips), 0)
    to = lax.broadcasted_iota(jnp.int32, (chips, GROUPS * chips), 1)
    total = jnp.zeros((width, GROUPS * chips), F32)
    for p in range(GROUPS):
        place = jnp.where(frm * GROUPS + p == to, 1.0, 0.0)
        moved = lax.dot_general(
            got, place, (((0,), (0,)), ((), ())),
            precision=lax.Precision.HIGHEST, preferred_element_type=F32,
        )
        total = total + moved[p * width : (p + 1) * width]
    out[...] = total

    for stage in range(7):
        count = chips >> ((stage + 1) // 2 if stage % 2 == 0 else stage // 2)
        some = bufs[stage].at[sub, pl.ds(0, count - 1)]
        pltpu.make_async_copy(some, some, send_sem.at[stage]).wait()
    some = snd.at[pl.ds(0, chips - 1)]
    pltpu.make_async_copy(some, some, send_sem.at[7]).wait()


def local(right_sides, diag_inverse, coupling, boundary, plane_map):
    chips = lax.axis_size("leaf")
    rows = right_sides.shape[3]
    part = rows // GROUPS
    width = right_sides.shape[0] * right_sides.shape[2]
    orders = [2 * chips * rows >> level for level in range(LEVELS)]
    d_cols, u_cols = sum(orders), sum(orders[1:])
    chunk = 2 * GROUPS * LANES
    stage_levels = [0, 0, 1, 1, 2, 2, 3]
    scratch = [
        pltpu.VMEM((2, rows, d_cols), F32),
        pltpu.VMEM((2, rows, u_cols), F32),
        pltpu.VMEM((2, GROUPS, 2 * rows, d_cols // GROUPS), BF16),
        pltpu.VMEM((2, GROUPS, 2 * rows, u_cols // GROUPS), BF16),
        pltpu.VMEM((chunk, chunk), BF16),
        *[pltpu.VMEM((2, chips >> level, part, LANES), F32) for level in stage_levels],
        pltpu.VMEM((sum(orders[:-1]), LANES), F32),
        pltpu.VMEM((orders[1] // GROUPS, LANES), F32),
        pltpu.VMEM((LEVELS, rows, LANES), F32),
        pltpu.VMEM((LEVELS * rows, LANES), F32),
        pltpu.VMEM((chips, 1, LANES), F32),
        pltpu.VMEM((chips, 1, LANES), F32),
        pltpu.SemaphoreType.DMA((LEVELS + 1,)),
        pltpu.SemaphoreType.DMA((16,)),
        pltpu.SemaphoreType.DMA((16,)),
    ]
    vmem, smem, whole = (
        pl.BlockSpec(memory_space=s) for s in (pltpu.VMEM, pltpu.SMEM, pl.ANY)
    )
    field = pl.pallas_call(
        functools.partial(body, chips, rows, orders),
        out_shape=jax.ShapeDtypeStruct((width, GROUPS * chips), F32),
        in_specs=[vmem, whole, whole, smem, smem],
        out_specs=vmem,
        scratch_shapes=scratch,
        compiler_params=pltpu.CompilerParams(
            has_side_effects=True, vmem_limit_bytes=44 << 20
        ),
    )(right_sides, diag_inverse, coupling, boundary, plane_map)
    return field.reshape(2, width // 2, GROUPS * chips)


def solution(mesh):
    in_specs = (
        P(None, None, None, ("leaf", "sub")),
        P(None, ("leaf", "sub"), None),
        P(None, ("leaf", "sub"), None),
        P(("leaf", "sub"), None),
        P(("leaf", "sub"), None),
    )
    out_specs = P(None, None, ("leaf", "sub"))
    return jax.shard_map(local, mesh=mesh, in_specs=in_specs, out_specs=out_specs, check_vma=False)
```

profile of v0, /device:TPU:0, one launch (start us, length us, event | category | flops | bytes accessed | tf_op | source)
XLA Modules:
  0.0 102.0 jit_solution(12259363483439667092)
XLA Ops:
  0.0 0.0 copy-start
  0.0 2.3 %copy-done = f32[2,48,11520]{2,1,0:T(8,128)S(1)} copy-done((f32[2,48,11520]{2,1,0:T(8,128)S(1)}, f32[2,48,11520]{2,1,0:T(8,128)}, u32[]{:S(2)}) %copy-start) | copy-done | bytes 4423704
  2.3 0.0 copy-start.1
  2.3 1.6 %copy-done.1 = f32[2,48,5376]{2,1,0:T(8,128)S(1)} copy-done((f32[2,48,5376]{2,1,0:T(8,128)S(1)}, f32[2,48,5376]{2,1,0:T(8,128)}, u32[]{:S(2)}) %copy-start.1) | copy-done | bytes 2064408
  3.8 0.0 copy-start.2
  3.8 0.8 copy-done.2
  4.7 0.0 copy-start.3
  4.7 0.7 copy-done.3
  5.4 0.0 copy-start.4
  5.4 0.7 copy-done.4
  6.1 95.2 %shard_map.55 = f32[32,192]{1,0:T(8,128)S(1)} custom-call(f32[2,4,16,48]{3,2,1,0:T(8,128)S(1)} %copy-done.2, f32[2,48,11520]{2,1,0:T(8,128)S(1)} %copy-done, f32[2,48,5376]{2,1,0:T(8,128)S(1)} %copy-done.1, s32[1,5376]{1,0:T(1,128)S(1)} %copy-done.3, s32[1,192]{1,0:T(1,128)S(1)} %copy-done.4), custom_call_target="tpu_custom_call" | custom-call | tf_op jit(solution)/shard_map/pallas_call | solution.py:334
  101.3 0.6 copy.7
Async XLA Ops:
  0.0 2.3 %copy-start = (f32[2,48,11520]{2,1,0:T(8,128)S(1)}, f32[2,48,11520]{2,1,0:T(8,128)}, u32[]{:S(2)}) copy-start(f32[2,48,11520]{2,1,0:T(8,128)} %d_hbm.1) | copy-start | bytes 13271044
  2.3 1.6 %copy-start.1 = (f32[2,48,5376]{2,1,0:T(8,128)S(1)}, f32[2,48,5376]{2,1,0:T(8,128)}, u32[]{:S(2)}) copy-start(f32[2,48,5376]{2,1,0:T(8,128)} %u_hbm.1) | copy-start | bytes 6193156
  3.8 0.8 copy-start.2
  4.7 0.7 copy-start.3
  5.4 0.7 copy-start.4
where the time goes:
time: 103 us; the launch traced here: 102 us
  Pallas kernels  95.2 us (92%)
  local copies, waits for them, and re-layouts  6.7 us (7%)
    pallas_call x1, Pallas kernels, local(): pl.pallas_call(functools.partial(body, chips, rows, orders), out_shape=ja...  95.2 us
    unnamed x11, local copies, waits for them, and re-layouts  6.7 us

commit v1 on v0

v1 whole, which is shorter than its diff:
```python
import functools

import jax
import jax.numpy as jnp
from jax import lax
from jax.experimental import pallas as pl
from jax.experimental.pallas import tpu as pltpu
from jax.sharding import PartitionSpec as P

LEVELS = 4
GROUPS = 3
LANES = 128
TILE = 256
SPAN = 4096
DIRECT = 2
CUTS = (0.35, 0.6)
MESH = pl.DeviceIdType.MESH
F32, BF16 = jnp.float32, jnp.bfloat16


def lane(rows):
    return lax.broadcasted_iota(jnp.int32, (rows, LANES), 1)


def roll(x, by):
    return pltpu.roll(x, by % LANES, 1)


def split(x):
    hi = x.astype(BF16)
    return hi, (x - hi.astype(F32)).astype(BF16)


def product(hi, lo, values):
    both = jnp.dot(hi, values, preferred_element_type=F32)
    rest = jnp.dot(lo, values[:, :LANES], preferred_element_type=F32)
    return both[:, :LANES] + both[:, LANES:] + rest


def fold(t, rows, width):
    half = width // 2
    m = 2 * rows
    y = t[:m] + roll(t[m : 2 * m], -width) + roll(t[2 * m :], -2 * width)
    a, b = y[:rows], y[rows:]
    at = lane(rows)
    swapped = jnp.where(at < half, -roll(b, -half), roll(b, half))
    return a + swapped


def pack(x, part, width):
    at = lane(part)
    return jnp.where(
        at < width,
        x[:part],
        jnp.where(
            at < 2 * width, roll(x[part : 2 * part], width), roll(x[2 * part :], 2 * width)
        ),
    )


def repeat(x, width):
    v = jnp.where(lane(x.shape[0]) < width, x, 0.0)
    v = v + roll(v, width)
    return v + roll(v, 2 * width)


def offsets(count):
    sizes = (max(count // 16, 1), min(max(count // 4, 1), 4), min(count, 4))
    steps = [
        (a, b, c)
        for a in range(sizes[0])
        for b in range(sizes[1])
        for c in range(sizes[2])
        if a or b or c
    ]
    hops = lambda step: sum(min(s, n - s) for s, n in zip(step, sizes))
    return sizes, sorted(steps, key=lambda step: -hops(step))


def body(
    chips, rows, orders, rs_hbm, d_hbm, u_hbm, bnd_hbm, pm_hbm, out, *rest
):
    (rs, bnd, pm, dv, uv, dp, uc, perm, qb, xb, ahead), rest = rest[:11], rest[11:]
    ups, bufs, rest = (None,) + rest[:3], rest[3:10], rest[10:]
    rt, sol, snd, rcv, load_sem, send_sem, recv_sem = rest
    leaf, sub = lax.axis_index("leaf"), lax.axis_index("sub")
    part = rows // GROUPS
    width = rs_hbm.shape[0] * rs_hbm.shape[2]
    tall = GROUPS * 2 * rows
    d_at = [sum(orders[:a]) for a in range(LEVELS + 1)]
    u_at = [0] + [sum(orders[1:a]) for a in range(1, LEVELS + 1)]
    k_at = [a // GROUPS for a in d_at]
    halves = [n // (2 * GROUPS) for n in orders]

    barrier = pltpu.get_barrier_semaphore()

    def chip(step, sizes, count):
        mine = lax.rem(leaf, count)
        z, x, y = mine // 16, lax.rem(mine // 4, 4), lax.rem(mine, 4)
        to = [lax.rem(at + s, n) for at, s, n in zip((z, x, y), step, sizes)]
        return leaf - mine + to[0] * 16 + to[1] * 4 + to[2]

    sizes, steps = offsets(chips)
    for step in steps:
        pl.semaphore_signal(
            barrier, inc=1, device_id=(chip(step, sizes, chips), sub), device_id_type=MESH
        )
    pl.semaphore_signal(barrier, inc=1, device_id=(leaf, 1 - sub), device_id_type=MESH)

    first = pltpu.make_async_copy(rs_hbm, rs, load_sem.at[LEVELS + 1])
    first.start()
    loads = []
    for level in range(LEVELS):
        span = pl.ds(d_at[level], orders[level])
        loads.append(
            pltpu.make_async_copy(d_hbm.at[:, :, span], dv.at[:, :, span], load_sem.at[level])
        )
    loads.append(pltpu.make_async_copy(u_hbm, uv, load_sem.at[LEVELS]))
    for i in range(bnd.shape[0]):
        pltpu.make_async_copy(
            bnd_hbm.at[:, pl.ds(i * LANES, LANES)], bnd.at[i], load_sem.at[LEVELS + 2]
        ).start()
    loads.append(pltpu.make_async_copy(bnd, bnd, load_sem.at[LEVELS + 2]))
    loads.append(pltpu.make_async_copy(pm_hbm, pm, load_sem.at[LEVELS + 3]))
    for load in (loads[LEVELS], *loads[:LEVELS], loads[-1]):
        load.start()

    def block(level):
        count = chips >> level
        return count, lax.rem(leaf, count)

    def send(stage, level, packed):
        buf = bufs[stage]
        count, mine = block(level)
        buf[sub, mine] = packed
        sizes, steps = offsets(count)

        def copy(to, core, sem):
            pltpu.make_async_remote_copy(
                src_ref=buf.at[sub, mine],
                dst_ref=buf.at[sub, mine],
                send_sem=send_sem.at[sem],
                recv_sem=recv_sem.at[sem],
                device_id=(to, core),
                device_id_type=MESH,
            ).start()

        for step in steps:
            to = chip(step, sizes, count)
            copy(to, sub, stage)
            if level >= DIRECT:
                copy(to, 1 - sub, 8 + stage)
        if level >= DIRECT:
            copy(leaf, 1 - sub, 8 + stage)

    def near(stage, level):
        buf = bufs[stage]
        count, _ = block(level)
        some = buf.at[sub, pl.ds(0, count - 1)]
        pltpu.make_async_copy(some, some, recv_sem.at[stage]).wait()
        if level < DIRECT:
            pltpu.make_async_remote_copy(
                src_ref=buf.at[sub],
                dst_ref=buf.at[sub],
                send_sem=send_sem.at[8 + stage],
                recv_sem=recv_sem.at[8 + stage],
                device_id=(leaf, 1 - sub),
                device_id_type=MESH,
            ).start()

    def far(stage, level):
        other = bufs[stage].at[1 - sub]
        pltpu.make_async_copy(other, other, recv_sem.at[8 + stage]).wait()

    def values(stage, level, p):
        return jnp.concatenate(split(bufs[stage][p].reshape(halves[level], LANES)), axis=1)

    def prepare_diag(level):
        loads[level].wait()
        chunk = perm.shape[0]
        for t in range(orders[level] // chunk):
            at = d_at[level] + t * chunk
            hi, lo = split(dv[:, :, at : at + chunk].reshape(2 * rows, chunk))
            both = jnp.concatenate([hi, lo], axis=0)
            moved = jnp.dot(both, perm[...], preferred_element_type=F32).astype(BF16)
            for p in range(2):
                for g in range(GROUPS):
                    to = k_at[level] + p * halves[level] + t * LANES
                    frm = (p * GROUPS + g) * LANES
                    for h in range(2):
                        dp[h, g, :, to : to + LANES] = moved[
                            h * 2 * rows : (h + 1) * 2 * rows, frm : frm + LANES
                        ]

    def both_halves(stage, level, part_of):
        near(stage, level)
        total = part_of(sub)
        far(stage, level)
        return total + part_of(1 - sub)

    def diag_product(stage, level):
        def part_of(p):
            at = pl.ds(pl.multiple_of(k_at[level] + p * halves[level], LANES), halves[level])
            return product(
                dp[0, :, :, at].reshape(tall, halves[level]),
                dp[1, :, :, at].reshape(tall, halves[level]),
                values(stage, level, p),
            )

        return fold(both_halves(stage, level, part_of), rows, width)

    def coupled(level, at, size):
        return product(
            ups[level][0, :, :, pl.ds(at, size)].reshape(tall, size),
            ups[level][1, :, :, pl.ds(at, size)].reshape(tall, size),
            xb[pl.ds(at, size), :],
        )

    def coupling_product(stage, level):
        up = level - 1

        def part_of(p):
            at = pl.multiple_of(k_at[up] + p * halves[up], LANES)
            xb[pl.ds(at, halves[up]), :] = values(stage, up, p)
            return coupled(level, at, halves[up])

        total = both_halves(stage, up, part_of)
        if level > 1:
            total = total + ahead[...]
        return fold(total, rows, width)

    def multiply_ahead(level):
        total = coupled(level, 0, k_at[1])
        for up in range(1, level - 1):
            total = total + coupled(level, k_at[up], k_at[up + 1] - k_at[up])
        ahead[...] = total

    def place_boundary():
        loads[LEVELS + 1].wait()
        index = bnd[...].reshape(bnd.shape[0], LANES)
        at, base, half = index, jnp.zeros_like(index), jnp.full_like(index, halves[0])
        for up in range(1, LEVELS - 1):
            below = index >= d_at[up]
            at = jnp.where(below, index - d_at[up], at)
            base = jnp.where(below, k_at[up], base)
            half = jnp.where(below, halves[up], half)
        owner = jnp.right_shift(at * ((1 << 21) // rows + 1), 21)
        inside = at - owner * rows
        group = jnp.right_shift(inside, 4)
        packed = base + (owner & 1) * half + jnp.right_shift(owner, 1) * part + (inside & 15)
        packed = jnp.transpose(group * SPAN + packed)
        for i in range(bnd.shape[0]):
            qb[i * LANES : (i + 1) * LANES, :] = jnp.broadcast_to(
                packed[:, i : i + 1], (LANES, LANES)
            )

    def split_coupling():
        loads[LEVELS].wait()
        for level in range(1, LEVELS):
            at = slice(u_at[level], u_at[level + 1])
            hi, lo = split(uv[:, :, at].reshape(2 * rows, orders[level]))
            uc[: 2 * rows, at] = hi
            uc[2 * rows :, at] = lo

    def select(level, begin, end):
        span = slice(u_at[level], u_at[level + 1])
        tiles = k_at[level] // TILE

        def one(t, carry):
            g = t // tiles
            k = pl.multiple_of((t - g * tiles) * TILE, TILE)
            want = lane(1) + (g * SPAN + k)
            q = qb[span, :]
            picks = [
                jnp.where(q == want + i * LANES, 1.0, 0.0).astype(BF16)
                for i in range(TILE // LANES)
            ]
            moved = jnp.dot(
                uc[:, span], jnp.concatenate(picks, axis=1), preferred_element_type=F32
            )
            hi, lo = split(moved[: 2 * rows] + moved[2 * rows :])
            ups[level][0, g, :, pl.ds(k, TILE)] = hi
            ups[level][1, g, :, pl.ds(k, TILE)] = lo
            return carry

        count = GROUPS * tiles
        lax.fori_loop(int(count * begin), int(count * end), one, 0)

    def keep(level, x):
        sol[level * rows : (level + 1) * rows, :] = repeat(x, width)

    first.wait()
    for level in range(LEVELS):
        rt[level, :, :width] = jnp.transpose(rs[:, level].reshape(width, rows))
    place_boundary()
    split_coupling()
    select(1, 0, CUTS[0])
    pl.semaphore_wait(barrier, chips)
    send(0, 0, pack(rt[0], part, width))

    chunk = perm.shape[0]
    col = lax.broadcasted_iota(jnp.int32, (1, chunk), 1)
    block_at = jnp.right_shift(col, 7)
    second = (block_at >= GROUPS).astype(jnp.int32)
    source = (
        jnp.right_shift(col & 127, 4) * (2 * rows)
        + second * rows
        + (block_at - GROUPS * second) * part
        + (col & 15)
    )
    row = lax.broadcasted_iota(jnp.int32, (chunk, chunk), 0)
    perm[...] = jnp.where(row == source, 1.0, 0.0).astype(BF16)
    prepare_diag(0)
    select(1, CUTS[0], CUTS[1])
    x = diag_product(0, 0)
    keep(0, x)
    send(1, 0, pack(x, part, width))
    select(1, CUTS[1], 1)
    prepare_diag(1)
    for level in range(1, LEVELS):
        z = rt[level] - coupling_product(2 * level - 1, level)
        send(2 * level, level, pack(z, part, width))
        if level + 1 < LEVELS:
            prepare_diag(level + 1)
            select(level + 1, 0, 0.5)
        x = diag_product(2 * level, level)
        keep(level, x)
        if level + 1 < LEVELS:
            send(2 * level + 1, level, pack(x, part, width))
            select(level + 1, 0.5, 1)
            multiply_ahead(level + 1)

    loads[-1].wait()
    at = lane(1)

    def pick(j, carry):
        r = [sol[pl.ds(pm[0, GROUPS * j + p], 1), :] for p in range(GROUPS)]
        snd[j] = jnp.where(at < width, r[0], jnp.where(at < 2 * width, r[1], r[2]))
        return carry

    lax.fori_loop(0, chips, pick, 0, unroll=8)
    rcv[leaf] = snd[leaf]
    sizes, steps = offsets(chips)
    for step in steps:
        to = chip(step, sizes, chips)
        pltpu.make_async_remote_copy(
            src_ref=snd.at[to],
            dst_ref=rcv.at[leaf],
            send_sem=send_sem.at[7],
            recv_sem=recv_sem.at[7],
            device_id=(to, sub),
            device_id_type=MESH,
        ).start()
    some = rcv.at[pl.ds(0, chips - 1)]
    pltpu.make_async_copy(some, some, recv_sem.at[7]).wait()
    got = rcv[...].reshape(chips, LANES)
    frm = lax.broadcasted_iota(jnp.int32, (chips, GROUPS * chips), 0)
    to = lax.broadcasted_iota(jnp.int32, (chips, GROUPS * chips), 1)
    total = jnp.zeros((width, GROUPS * chips), F32)
    for p in range(GROUPS):
        place = jnp.where(frm * GROUPS + p == to, 1.0, 0.0)
        moved = lax.dot_general(
            got, place, (((0,), (0,)), ((), ())),
            precision=lax.Precision.HIGHEST, preferred_element_type=F32,
        )
        total = total + moved[p * width : (p + 1) * width]
    out[...] = total

    for stage in range(7):
        level = (stage + 1) // 2 if stage % 2 == 0 else stage // 2
        some = bufs[stage].at[sub, pl.ds(0, (chips >> level) - 1)]
        pltpu.make_async_copy(some, some, send_sem.at[stage]).wait()
        some = bufs[stage].at[sub]
        pltpu.make_async_copy(some, some, send_sem.at[8 + stage]).wait()
    some = snd.at[pl.ds(0, chips - 1)]
    pltpu.make_async_copy(some, some, send_sem.at[7]).wait()


def local(right_sides, diag_inverse, coupling, boundary, plane_map):
    chips = lax.axis_size("leaf")
    rows = right_sides.shape[3]
    part = rows // GROUPS
    width = right_sides.shape[0] * right_sides.shape[2]
    orders = [2 * chips * rows >> level for level in range(LEVELS)]
    d_cols, u_cols = sum(orders), sum(orders[1:])
    chunk = 2 * GROUPS * LANES
    stage_levels = [0, 0, 1, 1, 2, 2, 3]
    packed = [sum(orders[:level]) // GROUPS for level in range(LEVELS)]
    scratch = [
        pltpu.VMEM(right_sides.shape, F32),
        pltpu.VMEM((u_cols // LANES, 1, LANES), jnp.int32),
        pltpu.SMEM(plane_map.shape, jnp.int32),
        pltpu.VMEM((2, rows, d_cols), F32),
        pltpu.VMEM((2, rows, u_cols), F32),
        pltpu.VMEM((2, GROUPS, 2 * rows, d_cols // GROUPS), BF16),
        pltpu.VMEM((4 * rows, u_cols), BF16),
        pltpu.VMEM((chunk, chunk), BF16),
        pltpu.VMEM((u_cols, LANES), jnp.int32),
        pltpu.VMEM((packed[-1], 2 * LANES), BF16),
        pltpu.VMEM((GROUPS * 2 * rows, LANES), F32),
        *[pltpu.VMEM((2, GROUPS, 2 * rows, k), BF16) for k in packed[1:]],
        *[pltpu.VMEM((2, chips >> level, part, LANES), F32) for level in stage_levels],
        pltpu.VMEM((LEVELS, rows, LANES), F32),
        pltpu.VMEM((LEVELS * rows, LANES), F32),
        pltpu.VMEM((chips, 1, LANES), F32),
        pltpu.VMEM((chips, 1, LANES), F32),
        pltpu.SemaphoreType.DMA((LEVELS + 4,)),
        pltpu.SemaphoreType.DMA((16,)),
        pltpu.SemaphoreType.DMA((16,)),
    ]
    vmem, hbm = (pl.BlockSpec(memory_space=s) for s in (pltpu.VMEM, pltpu.HBM))
    field = pl.pallas_call(
        functools.partial(body, chips, rows, orders),
        out_shape=jax.ShapeDtypeStruct((width, GROUPS * chips), F32),
        in_specs=[hbm] * 5,
        out_specs=vmem,
        scratch_shapes=scratch,
        compiler_params=pltpu.CompilerParams(
            collective_id=0, has_side_effects=True, vmem_limit_bytes=60 << 20
        ),
    )(right_sides, diag_inverse, coupling, boundary, plane_map)
    return field.reshape(2, width // 2, GROUPS * chips)


def solution(mesh):
    in_specs = (
        P(None, None, None, ("leaf", "sub")),
        P(None, ("leaf", "sub"), None),
        P(None, ("leaf", "sub"), None),
        P(("leaf", "sub"), None),
        P(("leaf", "sub"), None),
    )
    out_specs = P(None, None, ("leaf", "sub"))
    return jax.shard_map(local, mesh=mesh, in_specs=in_specs, out_specs=out_specs, check_vma=False)
```

time: 103 us -> 81.2 us (0.79)
  Pallas kernels: 95.2 us -> 79.6 us
  local copies, waits for them, and re-layouts: 6.7 us -> 1.38 us
    pallas_call x1, Pallas kernels: 95.2 us -> 79.6 us  [local(): pl.pallas_call(functools.partial(body, chips, rows, orders), out_shape=ja...]
    unnamed x11 -> x1, local copies, waits for them, and re-layouts: 6.7 us -> 1.38 us
where the time goes in v1:
time: 81.2 us; the launch traced here: 81 us
  Pallas kernels  79.6 us (98%)
  local copies, waits for them, and re-layouts  1.38 us (2%)
    pallas_call x1, Pallas kernels, local(): pl.pallas_call(functools.partial(body, chips, rows, orders), out_shape=ja...  79.6 us

profile of v1, /device:TPU:0, one launch (start us, length us, event | category | flops | bytes accessed | tf_op | source)
XLA Modules:
  0.0 81.0 jit_solution(1500209270332607283)
XLA Ops:
  0.0 79.6 %shard_map.55 = f32[32,192]{1,0:T(8,128)} custom-call(f32[2,4,16,48]{3,2,1,0:T(8,128)} %rs_hbm.1, f32[2,48,11520]{2,1,0:T(8,128)} %d_hbm.1, f32[2,48,5376]{2,1,0:T(8,128)} %u_hbm.1, s32[1,5376]{1,0:T(1,128)} %bnd_hbm.1, s32[1,192]{1,0:T(1,128)} %pm_hbm.1), custom_call_target="tpu_custom_call" | custom-call | tf_op jit(solution)/shard_map/pallas_call | solution.py:412
  79.6 1.4 %copy.7 = f32[2,16,192]{2,1,0:T(8,128)} copy(f32[2,16,192]{2,1,0:T(8,128)} %bitcast.1) | data formatting | bytes 49152

commit v2 on v1

--- a/solution.py
+++ b/solution.py
@@ -8,12 +8,21 @@
 from jax.sharding import PartitionSpec as P
 
 LEVELS = 4
+SENT = 12
 GROUPS = 3
 LANES = 128
-TILE = 256
+TILE = 512
 SPAN = 4096
 DIRECT = 2
-CUTS = (0.35, 0.6)
+PLAN = (
+    (),
+    ((1, 0, 3),),
+    ((1, 3, 12),),
+    ((2, 0, 9),),
+    ((2, 9, 18),),
+    ((3, 0, 9),),
+    ((3, 9, 21),),
+)
 MESH = pl.DeviceIdType.MESH
 F32, BF16 = jnp.float32, jnp.bfloat16
 
@@ -56,6 +65,28 @@
             at < 2 * width, roll(x[part : 2 * part], width), roll(x[2 * part :], 2 * width)
         ),
     )
+
+
+def squeeze(block, x, part, width):
+    last = [x[g * part + 8 : g * part + 16] for g in range(GROUPS)]
+    sub8 = lax.broadcasted_iota(jnp.int32, (8, LANES), 0)
+    spare = jnp.where(sub8 < 4, pltpu.roll(last[0], 4, 0), last[1])
+    free = lane(8) < GROUPS * width
+    top = jnp.where(free, block[:8], roll(spare, GROUPS * width))
+    low = jnp.where(free, block[8:], roll(pltpu.roll(last[2], 4, 0), GROUPS * width))
+    return top, low
+
+
+def restore(top, low, width):
+    at = lax.broadcasted_iota(jnp.int32, top.shape, 2)
+    sub8 = lax.broadcasted_iota(jnp.int32, top.shape, 1)
+    turn = lambda v, by: pltpu.roll(v, by % LANES, 2)
+    outer = jnp.where(at < width, turn(top, width), turn(low, 3 * width))
+    outer = pltpu.roll(outer, 4, 1)
+    inner = (at >= width) & (at < 2 * width)
+    moved = jnp.where(inner, turn(top, 2 * width), outer)
+    low = jnp.where(sub8 < 4, low, moved)
+    return jnp.concatenate([top, low], axis=1).reshape(-1, LANES)
 
 
 def repeat(x, width):
@@ -129,16 +160,18 @@
         count = chips >> level
         return count, lax.rem(leaf, count)
 
-    def send(stage, level, packed):
+    def send(stage, level, x):
         buf = bufs[stage]
         count, mine = block(level)
-        buf[sub, mine] = packed
+        top, low = squeeze(pack(x, part, width), x, part, width)
+        buf[sub, mine, :8] = top
+        buf[sub, mine, 8:] = low
         sizes, steps = offsets(count)
 
         def copy(to, core, sem):
             pltpu.make_async_remote_copy(
-                src_ref=buf.at[sub, mine],
-                dst_ref=buf.at[sub, mine],
+                src_ref=buf.at[sub, mine, pl.ds(0, SENT)],
+                dst_ref=buf.at[sub, mine, pl.ds(0, SENT)],
                 send_sem=send_sem.at[sem],
                 recv_sem=recv_sem.at[sem],
                 device_id=(to, core),
@@ -156,12 +189,12 @@
     def near(stage, level):
         buf = bufs[stage]
         count, _ = block(level)
-        some = buf.at[sub, pl.ds(0, count - 1)]
+        some = buf.at[sub, pl.ds(0, count - 1), pl.ds(0, SENT)]
         pltpu.make_async_copy(some, some, recv_sem.at[stage]).wait()
         if level < DIRECT:
             pltpu.make_async_remote_copy(
-                src_ref=buf.at[sub],
-                dst_ref=buf.at[sub],
+                src_ref=buf.at[sub, :, pl.ds(0, SENT)],
+                dst_ref=buf.at[sub, :, pl.ds(0, SENT)],
                 send_sem=send_sem.at[8 + stage],
                 recv_sem=recv_sem.at[8 + stage],
                 device_id=(leaf, 1 - sub),
@@ -169,11 +202,13 @@
             ).start()
 
     def far(stage, level):
-        other = bufs[stage].at[1 - sub]
+        other = bufs[stage].at[1 - sub, :, pl.ds(0, SENT)]
         pltpu.make_async_copy(other, other, recv_sem.at[8 + stage]).wait()
 
     def values(stage, level, p):
-        return jnp.concatenate(split(bufs[stage][p].reshape(halves[level], LANES)), axis=1)
+        buf = bufs[stage]
+        rows_of = restore(buf[p, :, :8], buf[p, :, 8:], width)
+        return jnp.concatenate(split(rows_of), axis=1)
 
     def prepare_diag(level):
         loads[level].wait()
@@ -262,7 +297,7 @@
             uc[: 2 * rows, at] = hi
             uc[2 * rows :, at] = lo
 
-    def select(level, begin, end):
+    def select_tiles(level, begin, end):
         span = slice(u_at[level], u_at[level + 1])
         tiles = k_at[level] // TILE
 
@@ -283,8 +318,11 @@
             ups[level][1, g, :, pl.ds(k, TILE)] = lo
             return carry
 
-        count = GROUPS * tiles
-        lax.fori_loop(int(count * begin), int(count * end), one, 0)
+        lax.fori_loop(begin, end, one, 0, unroll=3)
+
+    def select(wait):
+        for tiles in PLAN[wait]:
+            select_tiles(*tiles)
 
     def keep(level, x):
         sol[level * rows : (level + 1) * rows, :] = repeat(x, width)
@@ -292,11 +330,9 @@
     first.wait()
     for level in range(LEVELS):
         rt[level, :, :width] = jnp.transpose(rs[:, level].reshape(width, rows))
-    place_boundary()
-    split_coupling()
-    select(1, 0, CUTS[0])
+    select(0)
     pl.semaphore_wait(barrier, chips)
-    send(0, 0, pack(rt[0], part, width))
+    send(0, 0, rt[0])
 
     chunk = perm.shape[0]
     col = lax.broadcasted_iota(jnp.int32, (1, chunk), 1)
@@ -311,23 +347,25 @@
     row = lax.broadcasted_iota(jnp.int32, (chunk, chunk), 0)
     perm[...] = jnp.where(row == source, 1.0, 0.0).astype(BF16)
     prepare_diag(0)
-    select(1, CUTS[0], CUTS[1])
+    place_boundary()
+    split_coupling()
+    select(1)
     x = diag_product(0, 0)
     keep(0, x)
-    send(1, 0, pack(x, part, width))
-    select(1, CUTS[1], 1)
+    send(1, 0, x)
+    select(2)
     prepare_diag(1)
     for level in range(1, LEVELS):
         z = rt[level] - coupling_product(2 * level - 1, level)
-        send(2 * level, level, pack(z, part, width))
+        send(2 * level, level, z)
         if level + 1 < LEVELS:
             prepare_diag(level + 1)
-            select(level + 1, 0, 0.5)
+            select(2 * level + 1)
         x = diag_product(2 * level, level)
         keep(level, x)
         if level + 1 < LEVELS:
-            send(2 * level + 1, level, pack(x, part, width))
-            select(level + 1, 0.5, 1)
+            send(2 * level + 1, level, x)
+            select(2 * level + 2)
             multiply_ahead(level + 1)
 
     loads[-1].wait()
@@ -368,9 +406,9 @@
 
     for stage in range(7):
         level = (stage + 1) // 2 if stage % 2 == 0 else stage // 2
-        some = bufs[stage].at[sub, pl.ds(0, (chips >> level) - 1)]
+        some = bufs[stage].at[sub, pl.ds(0, (chips >> level) - 1), pl.ds(0, SENT)]
         pltpu.make_async_copy(some, some, send_sem.at[stage]).wait()
-        some = bufs[stage].at[sub]
+        some = bufs[stage].at[sub, :, pl.ds(0, SENT)]
         pltpu.make_async_copy(some, some, send_sem.at[8 + stage]).wait()
     some = snd.at[pl.ds(0, chips - 1)]
     pltpu.make_async_copy(some, some, send_sem.at[7]).wait()

time: 81.2 us -> 69.8 us (0.86)
  Pallas kernels: 79.6 us -> 68.2 us
    pallas_call x1, Pallas kernels: 79.6 us -> 68.2 us  [local(): pl.pallas_call(functools.partial(body, chips, rows, orders), out_shape=ja...]
where the time goes in v2:
time: 69.8 us; the launch traced here: 69.6 us
  Pallas kernels  68.2 us (98%)
  local copies, waits for them, and re-layouts  1.38 us (2%)
    pallas_call x1, Pallas kernels, local(): pl.pallas_call(functools.partial(body, chips, rows, orders), out_shape=ja...  68.2 us

profile of v2, /device:TPU:0, one launch (start us, length us, event | category | flops | bytes accessed | tf_op | source)
XLA Modules:
  0.0 69.6 jit_solution(14763676019602136086)
XLA Ops:
  0.0 68.2 %shard_map.55 = f32[32,192]{1,0:T(8,128)} custom-call(f32[2,4,16,48]{3,2,1,0:T(8,128)} %rs_hbm.1, f32[2,48,11520]{2,1,0:T(8,128)} %d_hbm.1, f32[2,48,5376]{2,1,0:T(8,128)} %u_hbm.1, s32[1,5376]{1,0:T(1,128)} %bnd_hbm.1, s32[1,192]{1,0:T(1,128)} %pm_hbm.1), custom_call_target="tpu_custom_call" | custom-call | tf_op jit(solution)/shard_map/pallas_call | solution.py:450
  68.2 1.4 %copy.7 = f32[2,16,192]{2,1,0:T(8,128)} copy(f32[2,16,192]{2,1,0:T(8,128)} %bitcast.1) | data formatting | bytes 49152

commit v3 on v2

--- a/solution.py
+++ b/solution.py
@@ -113,7 +113,7 @@
 ):
     (rs, bnd, pm, dv, uv, dp, uc, perm, qb, xb, ahead), rest = rest[:11], rest[11:]
     ups, bufs, rest = (None,) + rest[:3], rest[3:10], rest[10:]
-    rt, sol, snd, rcv, load_sem, send_sem, recv_sem = rest
+    place, rt, sol, snd, rcv, load_sem, send_sem, recv_sem = rest
     leaf, sub = lax.axis_index("leaf"), lax.axis_index("sub")
     part = rows // GROUPS
     width = rs_hbm.shape[0] * rs_hbm.shape[2]
@@ -125,17 +125,21 @@
 
     barrier = pltpu.get_barrier_semaphore()
 
-    def chip(step, sizes, count):
-        mine = lax.rem(leaf, count)
-        z, x, y = mine // 16, lax.rem(mine // 4, 4), lax.rem(mine, 4)
-        to = [lax.rem(at + s, n) for at, s, n in zip((z, x, y), step, sizes)]
-        return leaf - mine + to[0] * 16 + to[1] * 4 + to[2]
-
-    sizes, steps = offsets(chips)
-    for step in steps:
-        pl.semaphore_signal(
-            barrier, inc=1, device_id=(chip(step, sizes, chips), sub), device_id_type=MESH
-        )
+    def targets(count):
+        sizes, steps = offsets(count)
+        mine = leaf & (count - 1)
+        at = (mine >> 4, (mine >> 2) & 3, mine & 3)
+        axes = [
+            [((at[i] + s) & (n - 1)) * unit for s in range(n)]
+            for i, (n, unit) in enumerate(zip(sizes, (16, 4, 1)))
+        ]
+        axes[0] = [leaf - mine + z for z in axes[0]]
+        planes = [[z + x for x in axes[1]] for z in axes[0]]
+        return [(s, planes[s[0]][s[1]] + axes[2][s[2]]) for s in steps]
+
+    everyone = targets(chips)
+    for _, to in everyone:
+        pl.semaphore_signal(barrier, inc=1, device_id=(to, sub), device_id_type=MESH)
     pl.semaphore_signal(barrier, inc=1, device_id=(leaf, 1 - sub), device_id_type=MESH)
 
     first = pltpu.make_async_copy(rs_hbm, rs, load_sem.at[LEVELS + 1])
@@ -166,8 +170,6 @@
         top, low = squeeze(pack(x, part, width), x, part, width)
         buf[sub, mine, :8] = top
         buf[sub, mine, 8:] = low
-        sizes, steps = offsets(count)
-
         def copy(to, core, sem):
             pltpu.make_async_remote_copy(
                 src_ref=buf.at[sub, mine, pl.ds(0, SENT)],
@@ -178,8 +180,7 @@
                 device_id_type=MESH,
             ).start()
 
-        for step in steps:
-            to = chip(step, sizes, count)
+        for step, to in targets(count) if level else everyone:
             copy(to, sub, stage)
             if level >= DIRECT:
                 copy(to, 1 - sub, 8 + stage)
@@ -189,17 +190,25 @@
     def near(stage, level):
         buf = bufs[stage]
         count, _ = block(level)
-        some = buf.at[sub, pl.ds(0, count - 1), pl.ds(0, SENT)]
-        pltpu.make_async_copy(some, some, recv_sem.at[stage]).wait()
-        if level < DIRECT:
+
+        def arrive(blocks, sem):
+            some = buf.at[sub, pl.ds(0, blocks), pl.ds(0, SENT)]
+            pltpu.make_async_copy(some, some, recv_sem.at[sem]).wait()
+
+        def hand():
+            some = buf.at[sub, :, pl.ds(0, SENT)]
             pltpu.make_async_remote_copy(
-                src_ref=buf.at[sub, :, pl.ds(0, SENT)],
-                dst_ref=buf.at[sub, :, pl.ds(0, SENT)],
+                src_ref=some,
+                dst_ref=some,
                 send_sem=send_sem.at[8 + stage],
                 recv_sem=recv_sem.at[8 + stage],
                 device_id=(leaf, 1 - sub),
                 device_id_type=MESH,
             ).start()
+
+        arrive(count - 1, stage)
+        if level < DIRECT:
+            hand()
 
     def far(stage, level):
         other = bufs[stage].at[1 - sub, :, pl.ds(0, SENT)]
@@ -355,6 +364,10 @@
     send(1, 0, x)
     select(2)
     prepare_diag(1)
+    frm = lax.broadcasted_iota(jnp.int32, (chips, GROUPS * chips), 0)
+    to = lax.broadcasted_iota(jnp.int32, (chips, GROUPS * chips), 1)
+    for p in range(GROUPS):
+        place[p] = jnp.where(frm * GROUPS + p == to, 1.0, 0.0).astype(BF16)
     for level in range(1, LEVELS):
         z = rt[level] - coupling_product(2 * level - 1, level)
         send(2 * level, level, z)
@@ -378,9 +391,7 @@
 
     lax.fori_loop(0, chips, pick, 0, unroll=8)
     rcv[leaf] = snd[leaf]
-    sizes, steps = offsets(chips)
-    for step in steps:
-        to = chip(step, sizes, chips)
+    for _, to in everyone:
         pltpu.make_async_remote_copy(
             src_ref=snd.at[to],
             dst_ref=rcv.at[leaf],
@@ -392,16 +403,16 @@
     some = rcv.at[pl.ds(0, chips - 1)]
     pltpu.make_async_copy(some, some, recv_sem.at[7]).wait()
     got = rcv[...].reshape(chips, LANES)
-    frm = lax.broadcasted_iota(jnp.int32, (chips, GROUPS * chips), 0)
-    to = lax.broadcasted_iota(jnp.int32, (chips, GROUPS * chips), 1)
+    turned = jnp.transpose(got)
+    terms = []
+    for _ in range(3):
+        terms.append(turned.astype(BF16))
+        turned = turned - terms[-1].astype(F32)
     total = jnp.zeros((width, GROUPS * chips), F32)
     for p in range(GROUPS):
-        place = jnp.where(frm * GROUPS + p == to, 1.0, 0.0)
-        moved = lax.dot_general(
-            got, place, (((0,), (0,)), ((), ())),
-            precision=lax.Precision.HIGHEST, preferred_element_type=F32,
-        )
-        total = total + moved[p * width : (p + 1) * width]
+        term = jnp.concatenate([t[p * width : (p + 1) * width] for t in terms], axis=0)
+        moved = jnp.dot(term, place[p], preferred_element_type=F32)
+        total = total + (moved[2 * width :] + moved[width : 2 * width] + moved[:width])
     out[...] = total
 
     for stage in range(7):
@@ -438,6 +449,7 @@
         pltpu.VMEM((GROUPS * 2 * rows, LANES), F32),
         *[pltpu.VMEM((2, GROUPS, 2 * rows, k), BF16) for k in packed[1:]],
         *[pltpu.VMEM((2, chips >> level, part, LANES), F32) for level in stage_levels],
+        pltpu.VMEM((GROUPS, chips, GROUPS * chips), BF16),
         pltpu.VMEM((LEVELS, rows, LANES), F32),
         pltpu.VMEM((LEVELS * rows, LANES), F32),
         pltpu.VMEM((chips, 1, LANES), F32),

time: 69.8 us -> 69.3 us (level)
  no operation moved by 1% of the time
where the time goes in v3:
time: 69.3 us; the launch traced here: 69.1 us
  Pallas kernels  67.7 us (98%)
  local copies, waits for them, and re-layouts  1.38 us (2%)
    pallas_call x1, Pallas kernels, local(): pl.pallas_call(functools.partial(body, chips, rows, orders), out_shape=ja...  67.7 us

profile of v3, /device:TPU:0, one launch (start us, length us, event | category | flops | bytes accessed | tf_op | source)
XLA Modules:
  0.0 69.1 jit_solution(15883504655462913307)
XLA Ops:
  0.0 67.7 %shard_map.55 = f32[32,192]{1,0:T(8,128)} custom-call(f32[2,4,16,48]{3,2,1,0:T(8,128)} %rs_hbm.1, f32[2,48,11520]{2,1,0:T(8,128)} %d_hbm.1, f32[2,48,5376]{2,1,0:T(8,128)} %u_hbm.1, s32[1,5376]{1,0:T(1,128)} %bnd_hbm.1, s32[1,192]{1,0:T(1,128)} %pm_hbm.1), custom_call_target="tpu_custom_call" | custom-call | tf_op jit(solution)/shard_map/pallas_call | solution.py:462
  67.7 1.4 %copy.7 = f32[2,16,192]{2,1,0:T(8,128)} copy(f32[2,16,192]{2,1,0:T(8,128)} %bitcast.1) | data formatting | bytes 49152
